TPU v7x, 128 devices: a whole 4x4x4 slice. The times are simulated.
128 devices in a mesh: seq: 8 (over z, core), tp: 16 (over x, y).
Axes of the slice: x: 4, y: 4, z: 4, core: 2. Of those that a mesh axis runs over, the one named last changes fastest.
Arguments:
- sequence_in: bfloat16 [1536, 4096], P('tp', 'seq')
- conv_weight: bfloat16 [3, 1536, 3, 1536], P(None, 'tp')
- norm_gain: float32 [3, 1536], P(None, 'tp'), may hold values from 0.1 to 1.9
- tissue_scale: float32 [367, 1536], replicated, may hold values from 0.3 to 3
- donor_offset: int32 [2048], P('seq'), may hold values from 0 to 511
- acceptor_owner: int32 [2048, 1], P('seq'), may hold values from 0 to 7; in each aligned block of 256 rows (0 to 255, 256 to 511, ...) at most 128 rows name the same one
- acceptor_offset: int32 [2048], P('seq'), may hold values from 0 to 511
- tissue: int32 [2048], P('seq'), may hold values from 0 to 366
- tower_grad: float32 [1536, 4096], P('tp', 'seq'), may hold values from -6 to 6
- score_grad: float32 [2048], P('seq'), may hold values from -24 to 24
Outputs:
- scores: float32 [2048], P('seq')
- input_grad: float32 [1536, 4096], P('tp', 'seq')
- weight_grad: float32 [3, 1536, 3, 1536], P(None, 'tp')
- gain_grad: float32 [3, 1536], P(None, 'tp')
Inputs may be any that keep to these rules, and one draw needn't show every extreme that they name: `acceptor_owner`: among the 256 junctions of one index of seq, at most 128 have their acceptor on one index of seq.
All inputs are finite; a program needn't handle non-finite values.
Results may differ from a plain program's by a relative error of at most 0.025.
Values may be sent and summed in bfloat16 or wider, within the bound.
A program may use at most 128 MiB of HBM per device.

v0:
```python
import math
import jax
import jax.numpy as jnp
from jax import lax
from jax.sharding import PartitionSpec as P

CHANNELS = 1536
LAYERS = 3
CAP = 128
EPSILON = 1e-06


def with_halo(x, sides, width):
    for axis, dim in sides:
        count, length = (lax.axis_size(axis), x.shape[dim])
        up = [(i, (i + 1) % count) for i in range(count - 1)]
        down = [(j, i) for i, j in up]
        last = lax.slice_in_dim(x, length - width, length, axis=dim)
        initial = lax.slice_in_dim(x, 0, width, axis=dim)
        before = lax.ppermute(last, axis, up)
        after = lax.ppermute(initial, axis, down)
        x = jnp.concatenate([before, x, after], axis=dim)
    return x


def gelu_fn(value):
    return jax.nn.gelu(value, approximate=True)


def widen(block, width):
    return with_halo(block, (("seq", 1),), width)


def forward_taps(weights, padded, reach, length):
    total = jnp.zeros((weights.shape[0], length), jnp.float32)
    for tap in range(3):
        total = total + jnp.dot(
            weights[:, tap, :],
            padded[:, tap * reach : tap * reach + length],
            preferred_element_type=jnp.float32,
        )
    return total


def backward_taps(weights, grad_pad, reach, length):
    total = jnp.zeros((weights.shape[2], length), jnp.float32)
    for tap in range(3):
        total = total + lax.dot_general(
            weights[:, tap, :],
            grad_pad[:, (2 - tap) * reach : (2 - tap) * reach + length],
            (((0,), (0,)), ((), ())),
            preferred_element_type=jnp.float32,
        )
    return total


def weight_taps(padded, grad_bf, reach, length):
    blocks = []
    for tap in range(3):
        blocks.append(
            lax.dot_general(
                grad_bf,
                padded[:, tap * reach : tap * reach + length],
                (((1,), (1,)), ((), ())),
                preferred_element_type=jnp.float32,
            )
        )
    return jnp.stack(blocks, axis=1)


def local(
    sequence_in,
    conv_weight,
    norm_gain,
    tissue_scale,
    donor_offset,
    acceptor_owner,
    acceptor_offset,
    tissue,
    tower_grad,
    score_grad,
):
    local_ch = sequence_in.shape[0]
    length = sequence_in.shape[1]
    seq_count = lax.axis_size("seq")
    state = sequence_in
    stored = []
    for layer in range(LAYERS):
        reach = 2 ** (layer + 3)
        stream = state.astype(jnp.float32)
        power = lax.psum(jnp.sum(stream * stream, axis=0), "tp") / CHANNELS
        inverse = 1.0 / jnp.sqrt(power + EPSILON)
        pre_act = stream * inverse[None, :] * norm_gain[layer][:, None]
        hidden = gelu_fn(pre_act).astype(jnp.bfloat16)
        padded = widen(hidden, reach)
        weights = conv_weight[layer]
        gathered = padded

        def fold_inputs(total, piece, start, weights=weights, reach=reach):
            return forward_taps(weights, piece, reach, length)

        mixed = fold_inputs(
            jnp.zeros((local_ch, length), jnp.float32),
            lax.all_gather(padded, "tp", axis=0, tiled=True),
            jnp.int32(0),
        )
        stored.append((state, inverse, pre_act, gathered))
        state = (stream + mixed).astype(jnp.bfloat16)
    owner = acceptor_owner[:, 0]
    member = (owner[:, None] == jnp.arange(seq_count, dtype=jnp.int32)[None, :]).astype(jnp.int32)
    slot = jnp.sum(jnp.cumsum(member, axis=0) * member, axis=1) - 1
    requests = jnp.zeros((seq_count, CAP), jnp.int32).at[owner, slot].set(acceptor_offset)
    rows_view = state.T
    offsets = lax.all_to_all(requests, "seq", split_axis=0, concat_axis=0, tiled=True)
    picked = rows_view[offsets]
    returned = lax.all_to_all(picked, "seq", split_axis=0, concat_axis=0, tiled=True)
    accept_cols = returned[owner, slot].astype(jnp.float32)
    donor_cols = rows_view[donor_offset].astype(jnp.float32)
    chan_start = lax.axis_index("tp") * local_ch
    local_table = lax.dynamic_slice_in_dim(tissue_scale, chan_start, local_ch, 1)
    tissue_hit = (
        tissue[:, None] == jnp.arange(tissue_scale.shape[0], dtype=jnp.int32)[None, :]
    ).astype(jnp.float32)
    tissue_rows = jnp.dot(tissue_hit, local_table, precision=lax.Precision.HIGHEST)
    root = math.sqrt(CHANNELS)
    partial_scores = jnp.sum(donor_cols * accept_cols * tissue_rows, axis=1) / root
    scores = lax.psum(partial_scores, "tp")
    weight_j = score_grad / root
    donor_back = weight_j[:, None] * accept_cols * tissue_rows
    accept_back = weight_j[:, None] * donor_cols * tissue_rows
    outgoing = jnp.zeros((seq_count, CAP, local_ch), jnp.float32).at[owner, slot].set(accept_back)
    incoming = lax.all_to_all(
        outgoing.astype(jnp.bfloat16), "seq", split_axis=0, concat_axis=0, tiled=True
    ).astype(outgoing.dtype)
    upstream = tower_grad.at[:, donor_offset].add(donor_back.T)
    upstream = upstream.at[:, offsets.reshape(-1)].add(incoming.reshape(-1, local_ch).T)
    weight_list = [None] * LAYERS
    gain_list = [None] * LAYERS
    for layer in reversed(range(LAYERS)):
        reach = 2 ** (layer + 3)
        old_state, inverse, pre_act, gathered = stored[layer]
        stream = old_state.astype(jnp.float32)
        grad_bf = upstream.astype(jnp.bfloat16)
        grad_pad = widen(grad_bf, reach)
        weights = conv_weight[layer]

        def term_rows(start, count, weights=weights, grad_pad=grad_pad, reach=reach):
            return backward_taps(weights, grad_pad, reach, length)

        back_hidden = lax.psum_scatter(
            term_rows(jnp.int32(0), local_ch * lax.axis_size("tp")).astype(jnp.bfloat16),
            "tp",
            scatter_dimension=0,
            tiled=True,
        ).astype(jnp.float32)

        def fold_weights(total, piece, start, grad_bf=grad_bf, reach=reach):
            return weight_taps(piece, grad_bf, reach, length)

        weight_term = fold_weights(
            jnp.zeros((local_ch, 3, CHANNELS), jnp.float32),
            lax.all_gather(gathered, "tp", axis=0, tiled=True),
            jnp.int32(0),
        )
        weight_list[layer] = lax.psum(weight_term.astype(jnp.bfloat16), "seq").astype(jnp.float32)
        _, gelu_back = jax.vjp(gelu_fn, pre_act)
        back_pre = gelu_back(back_hidden)[0]
        gain_list[layer] = jnp.sum(back_pre * stream * inverse[None, :], axis=1)
        back_norm = back_pre * norm_gain[layer][:, None]
        inner = lax.psum(jnp.sum(back_norm * stream, axis=0), "tp")
        upstream = (
            upstream
            + inverse[None, :] * back_norm
            - stream * (inverse**3)[None, :] * inner[None, :] / CHANNELS
        )
    gain_grad = lax.psum(jnp.stack(gain_list), "seq")
    return (scores, upstream, jnp.stack(weight_list), gain_grad)


def solution(mesh):
    return jax.shard_map(
        local,
        mesh=mesh,
        in_specs=(
            P("tp", "seq"),
            P(None, "tp", None, None),
            P(None, "tp"),
            P(),
            P("seq"),
            P("seq", None),
            P("seq"),
            P("seq"),
            P("tp", "seq"),
            P("seq"),
        ),
        out_specs=(P("seq"), P("tp", "seq"), P(None, "tp", None, None), P(None, "tp")),
        check_vma=False,
    )
```

profile of v0, /device:TPU:0, one launch (start us, length us, event | category | flops | bytes accessed | tf_op | source)
XLA Modules:
  0.0 813.4 jit_solution(14602728577334916671)
XLA Ops:
  9.6 40.8 %psum.77 = f32[512]{0:T(512)S(1)} all-reduce(f32[512]{0:T(512)S(1)} %fusion.133), channel_id=1, replica_groups=mesh['seq'=8,'tp'=16] {'tp'}, use_global_device_ids=true, to_apply=%region_1.0 | all-reduce | flops 512 | bytes 4096 | tf_op jit(solution)/shard_map/psum | solution.py:91
  54.7 3.9 collective-permute-done.1
  62.6 40.5 %all-gather.4.cloned.1.call-done = bf16[1536,528]{1,0:T(8,128)(2,1)} async-done(((bf16[96,528]{1,0:T(8,128)(2,1)}), bf16[1536,528]{1,0:T(8,128)(2,1)}) %all-gather.4.cloned.1.call-update) | async-done | bytes 1622032 | tf_op jit(solution)/shard_map/all_gather | solution.py:104
  108.2 38.1 %psum.78 = f32[512]{0:T(512)S(1)} all-reduce(f32[512]{0:T(512)S(1)} %get-tuple-element.50), channel_id=1, replica_groups=mesh['seq'=8,'tp'=16] {'tp'}, use_global_device_ids=true, to_apply=%region_3.0 | all-reduce | flops 512 | bytes 4096 | tf_op jit(solution)/shard_map/psum | solution.py:91
  149.7 3.6 collective-permute-done.3
  154.1 42.9 %all-gather.6.cloned.1.call-done = bf16[1536,544]{1,0:T(8,128)(2,1)} async-done(((bf16[96,544]{1,0:T(8,128)(2,1)}), bf16[1536,544]{1,0:T(8,128)(2,1)}) %all-gather.6.cloned.1.call-update) | async-done | bytes 1671184 | tf_op jit(solution)/shard_map/all_gather | solution.py:104
  200.5 38.3 %psum.79 = f32[512]{0:T(512)S(1)} all-reduce(f32[512]{0:T(512)S(1)} %get-tuple-element.52), channel_id=1, replica_groups=mesh['seq'=8,'tp'=16] {'tp'}, use_global_device_ids=true, to_apply=%region_5.0 | all-reduce | flops 512 | bytes 4096 | tf_op jit(solution)/shard_map/psum | solution.py:91
  248.8 38.6 %scatter_fusion = s32[8,128]{1,0:T(8,128)} fusion(s32[8,128]{1,0:T(8,128)} %broadcast.150, s32[256]{0:T(256)S(1)} %bitcast.150, s32[256]{0:T(256)} %param.16), kind=kCustom, calls=%fused_computation.3 | custom fusion | bytes 5120 | tf_op jit(solution)/shard_map/scatter | solution.py:112
  287.5 6.3 all-to-all-start
  294.4 4.6 all-to-all-done
  312.7 5.7 all-to-all-done.1
  322.2 16.8 %scatter_fusion.2 = f32[8,128,96]{2,1,0:T(8,128)S(1)} fusion(f32[8,128,96]{2,1,0:T(8,128)S(1)} %broadcast_in_dim.5, s32[256]{0:T(256)S(1)} %bitcast.151, f32[256,96]{1,0:T(8,128)} %copy.100), kind=kCustom, calls=%fused_computation.5 | custom fusion | bytes 296960 | tf_op jit(solution)/shard_map/scatter | solution.py:131
  339.8 4.0 all-to-all-start.2
  346.4 4.3 all-to-all-done.2
  351.7 6.3 scatter_fusion.3
  368.0 71.8 %reduce-scatter.4.cloned.1.call-done = bf16[96,512]{1,0:T(8,128)(2,1)} async-done(((bf16[1536,512]{1,0:T(8,128)(2,1)}), bf16[96,512]{1,0:T(8,128)(2,1)}) %reduce-scatter.4.cloned.1.call-update) | async-done | bytes 98320 | tf_op jit(solution)/shard_map/reduce_scatter | solution.py:150
  441.0 38.1 %psum.81 = f32[512]{0:T(512)S(1)} all-reduce(f32[512]{0:T(512)S(1)} %get-tuple-element.7), channel_id=1, replica_groups=mesh['seq'=8,'tp'=16] {'tp'}, use_global_device_ids=true, to_apply=%region_17.18 | all-reduce | flops 512 | bytes 4096 | tf_op jit(solution)/shard_map/psum | solution.py:170
  499.2 64.4 %reduce-scatter.6.cloned.1.call-done = bf16[96,512]{1,0:T(8,128)(2,1)} async-done(((bf16[1536,512]{1,0:T(8,128)(2,1)}), bf16[96,512]{1,0:T(8,128)(2,1)}) %reduce-scatter.6.cloned.1.call-update) | async-done | bytes 98320 | tf_op jit(solution)/shard_map/reduce_scatter | solution.py:150
  564.9 38.3 %psum.82 = f32[512]{0:T(512)S(1)} all-reduce(f32[512]{0:T(512)S(1)} %get-tuple-element.5), channel_id=1, replica_groups=mesh['seq'=8,'tp'=16] {'tp'}, use_global_device_ids=true, to_apply=%region_20.21 | all-reduce | flops 512 | bytes 4096 | tf_op jit(solution)/shard_map/psum | solution.py:170
  618.1 55.7 %all-reduce.4.cloned.1.call-done = (bf16[1,96,3,1536]{3,1,2,0:T(8,128)(2,1)}, bf16[1,96,3,1536]{3,1,2,0:T(8,128)(2,1)}, bf16[1,96,3,1536]{3,1,2,0:T(8,128)(2,1)}) async-done(((bf16[1,96,3,1536]{3,1,2,0:T(8,128)(2,1)}, bf16[1,96,3,1536]{3,1,2,0:T(8,128)(2,1)}, bf16[1,96,3,1536]{3,1,2,0:T(8,128)(2,1)}), (bf16[1,96,3,1536]{3,1,2,0:T(8,128)(2,1)}, bf16[1,96,3,1536]{3,1,2,0:T(8,128)(2,1)}, ...) | async-done | bytes 2654224 | tf_op jit(solution)/shard_map/psum | solution.py:165
  673.8 4.5 maximum_convert_fusion
  678.3 72.7 %reduce-scatter.8.cloned.1.call-done = bf16[96,512]{1,0:T(8,128)(2,1)} async-done(((bf16[1536,512]{1,0:T(8,128)(2,1)}), bf16[96,512]{1,0:T(8,128)(2,1)}) %reduce-scatter.8.cloned.1.call-update) | async-done | bytes 98320 | tf_op jit(solution)/shard_map/reduce_scatter | solution.py:150
  752.3 13.7 %psum.87 = f32[3,96]{1,0:T(4,128)} all-reduce(f32[3,96]{1,0:T(4,128)S(1)} %pad_maximum_fusion.15), channel_id=1, replica_groups=mesh['seq'=8,'tp'=16] {'seq'}, use_global_device_ids=true, to_apply=%region_30.31 | all-reduce | flops 288 | bytes 2304 | tf_op jit(solution)/shard_map/psum | solution.py:176
  766.1 38.6 %all-reduce = (f32[256]{0:T(256)}, f32[512]{0:T(512)S(1)}) all-reduce(f32[256]{0:T(256)S(1)} %broadcast_multiply_fusion.1, f32[512]{0:T(512)S(1)} %get-tuple-element.9), channel_id=1, replica_groups=mesh['seq'=8,'tp'=16] {'tp'}, use_global_device_ids=true, to_apply=%region_11.12 | all-reduce | flops 768 | bytes 6144 | tf_op jit(solution)/shard_map/psum | solution.py:127
  (192 shorter events, 105.7 us)
Async XLA Ops:
  7.2 313.2 %copy-start = (f32[367,1536]{1,0:T(8,128)S(1)}, f32[367,1536]{1,0:T(8,128)}, u32[]{:S(2)}) copy-start(f32[367,1536]{1,0:T(8,128)} %param.13) | copy-start | bytes 6764548
  7.2 96.0 %all-gather.4.cloned.1.call-start = ((), (), s32[]{:S(2)}) async-start(), calls=%async_computation.6 | async-start | bytes 2088960 | tf_op jit(solution)/shard_map/all_gather | solution.py:104
  8.7 138.3 %copy-start.24 = (f32[96]{0:T(128)}, f32[96]{0:T(128)S(1)}, u32[]{:S(2)}) copy-start(f32[96]{0:T(128)S(1)} %get-tuple-element.47) | copy-start | bytes 1156
  52.1 2.6 collective-permute-start
  53.4 5.2 collective-permute-start.1
  59.4 137.7 %all-gather.6.cloned.1.call-start = ((), (), s32[]{:S(2)}) async-start(), calls=%async_computation.7 | async-start | bytes 2088960 | tf_op jit(solution)/shard_map/all_gather | solution.py:104
  147.1 2.6 collective-permute-start.2
  148.4 4.9 collective-permute-start.3
  154.1 145.0 %all-gather.8.cloned.1.call-start = ((), (), s32[]{:S(2)}) async-start(), calls=%async_computation.8 | async-start | bytes 2088960 | tf_op jit(solution)/shard_map/all_gather | solution.py:104
  240.3 2.6 collective-permute-start.4
  241.6 4.9 collective-permute-start.5
  287.5 11.6 %all-to-all-start = ((s32[8,1,128]{2,1,0:T(1,128)}), s32[8,1,128]{2,1,0:T(1,128)S(1)}, u32[]{:S(2)}, u32[]{:S(2)}) async-start(s32[8,1,128]{2,1,0:T(1,128)} %bitcast.27), calls=%async_computation | async-start | bytes 8192 | tf_op jit(solution)/shard_map/all_to_all | solution.py:114
  308.3 10.1 %all-to-all-start.1 = ((bf16[8,128,96]{1,2,0:T(8,128)(2,1)}), bf16[8,128,96]{1,2,0:T(8,128)(2,1)S(1)}, u32[]{:S(2)}, u32[]{:S(2)}) async-start(bf16[8,128,96]{1,2,0:T(8,128)(2,1)} %copy.95), calls=%async_computation.1 | async-start | bytes 393216 | tf_op jit(solution)/shard_map/all_to_all | solution.py:116
  339.8 10.8 %all-to-all-start.2 = ((bf16[8,128,96]{1,2,0:T(8,128)(2,1)}), bf16[8,128,96]{1,2,0:T(8,128)(2,1)}, u32[]{:S(2)}, u32[]{:S(2)}) async-start(bf16[8,128,96]{1,2,0:T(8,128)(2,1)} %copy.101), calls=%async_computation.2 | async-start | bytes 393216 | tf_op jit(solution)/shard_map/all_to_all | solution.py:132
  343.9 95.9 %reduce-scatter.4.cloned.1.call-start = ((), (), s32[]{:S(2)}) async-start(), calls=%async_computation.9 | async-start | bytes 1671168 | tf_op jit(solution)/shard_map/reduce_scatter | solution.py:150
  358.1 5.6 collective-permute-start.7
  362.4 3.6 collective-permute-start.6
  367.8 195.9 %reduce-scatter.6.cloned.1.call-start = ((), (), s32[]{:S(2)}) async-start(), calls=%async_computation.10 | async-start | bytes 1671168 | tf_op jit(solution)/shard_map/reduce_scatter | solution.py:150
  481.1 4.3 collective-permute-start.9
  484.1 4.9 collective-permute-start.8
  490.8 183.0 %all-reduce.4.cloned.1.call-start = ((), (), s32[]{:S(2)}) async-start(), calls=%async_computation.12 | async-start | bytes 5308416 | tf_op jit(solution)/shard_map/psum | solution.py:165
  609.3 141.7 %reduce-scatter.8.cloned.1.call-start = ((), (), s32[]{:S(2)}) async-start(), calls=%async_computation.11 | async-start | bytes 1671168 | tf_op jit(solution)/shard_map/reduce_scatter | solution.py:150
  609.5 3.2 collective-permute-start.11
  611.4 4.9 collective-permute-start.10
  (31 other events, 1319.9 us)
Sparse Core Ops, SparseCore 0:
  59.5 43.5 all-gather.3
  154.2 42.8 all-gather.5
  247.4 42.8 all-gather.7
  367.9 71.7 reduce-scatter.3
  490.9 72.7 reduce-scatter.5
  609.5 64.2 all-reduce.3
  677.0 73.9 reduce-scatter.7
where the time goes:
time: 816 us; the launch traced here: 813 us
  waiting for transfers between devices  381 us (47%)
  blocking collectives  246 us (30%)
  local copies, waits for them, and re-layouts  71.9 us (9%)
  matrix products  35.4 us (4%)
  other arithmetic  32.8 us (4%)
  starting transfers between devices  30.9 us (4%)
  between operations  14.9 us (2%)
    reduce_scatter x3, waiting for transfers between devices, local(): lax.psum_scatter(term_rows(jnp.int32(0), local_ch * lax.axis_size('tp'))....  209 us
    psum x3, blocking collectives, local(): power = lax.psum(jnp.sum(stream * stream, axis=0), 'tp') / CHANNELS  117 us
    all_gather x3, waiting for transfers between devices, local(): lax.all_gather(padded, 'tp', axis=0, tiled=True)  83.4 us
    psum x2, blocking collectives, local(): inner = lax.psum(jnp.sum(back_norm * stream, axis=0), 'tp')  76.5 us
    psum x1, waiting for transfers between devices, local(): lax.psum(weight_term.astype(jnp.bfloat16), 'seq').astype(jnp.float32)  55.7 us
    psum x1, blocking collectives, local(): scores = lax.psum(partial_scores, 'tp')  38.6 us
    scatter x1, local copies, waits for them, and re-layouts, local(): jnp.zeros((seq_count, CAP), jnp.int32).at[owner, slot].set(acceptor_offset)  38.6 us
    ppermute x6, waiting for transfers between devices, with_halo(): after = lax.ppermute(initial, axis, down)  18.6 us
  transfers between devices with their start and end apart: 22, of which 15 were waited for; matrix products, arithmetic and copies ran while one was open for 8% of the time, Pallas kernels for 0%

commit v1 on v0

--- a/solution.py
+++ b/solution.py
@@ -101,7 +101,9 @@
 
         mixed = fold_inputs(
             jnp.zeros((local_ch, length), jnp.float32),
-            lax.all_gather(padded, "tp", axis=0, tiled=True),
+            jnp.concatenate(
+                lax.all_to_all(jnp.stack([padded] * lax.axis_size("tp")), "tp", 0, 0), axis=0
+            ),
             jnp.int32(0),
         )
         stored.append((state, inverse, pre_act, gathered))

time: 816 us -> 888 us (1.088)
  waiting for transfers between devices: 381 us -> 420 us
  starting transfers between devices: 30.9 us -> 48.7 us
    all_to_all x0 -> x3, waiting for transfers between devices: none -> 80.4 us  [local(): lax.all_to_all(jnp.stack([padded] * lax.axis_size('tp')), 'tp', 0, 0)]
    all_gather x3, waiting for transfers between devices: 83.4 us -> 42.3 us  [local(): lax.all_gather(gathered, 'tp', axis=0, tiled=True)]
    all_to_all x0 -> x3, starting transfers between devices: none -> 13.5 us  [local(): lax.all_to_all(jnp.stack([padded] * lax.axis_size('tp')), 'tp', 0, 0)]
    ppermute x6, waiting for transfers between devices: 18.6 us -> 7.51 us  [with_halo(): after = lax.ppermute(initial, axis, down)]
  transfers between devices with their start and end apart: 22 -> 25, of which waited for: 15 -> 17; matrix products, arithmetic and copies ran while one was open for 8% -> 9% of each run, Pallas kernels for 0% -> 0%
where the time goes in v1:
time: 888 us; the launch traced here: 885 us
  waiting for transfers between devices  420 us (47%)
  blocking collectives  244 us (27%)
  local copies, waits for them, and re-layouts  80.6 us (9%)
  starting transfers between devices  48.7 us (5%)
  matrix products  42.4 us (5%)
  other arithmetic  34.2 us (4%)
  between operations  14.9 us (2%)
    reduce_scatter x3, waiting for transfers between devices, local(): lax.psum_scatter(term_rows(jnp.int32(0), local_ch * lax.axis_size('tp'))....  217 us
    psum x3, blocking collectives, local(): power = lax.psum(jnp.sum(stream * stream, axis=0), 'tp') / CHANNELS  115 us
    all_to_all x3, waiting for transfers between devices, local(): lax.all_to_all(jnp.stack([padded] * lax.axis_size('tp')), 'tp', 0, 0)  80.4 us
    psum x2, blocking collectives, local(): inner = lax.psum(jnp.sum(back_norm * stream, axis=0), 'tp')  76.4 us
    psum x1, waiting for transfers between devices, local(): lax.psum(weight_term.astype(jnp.bfloat16), 'seq').astype(jnp.float32)  58.8 us
    all_gather x3, waiting for transfers between devices, local(): lax.all_gather(gathered, 'tp', axis=0, tiled=True)  42.3 us
    scatter x1, local copies, waits for them, and re-layouts, local(): jnp.zeros((seq_count, CAP), jnp.int32).at[owner, slot].set(acceptor_offset)  38.7 us
    psum x1, blocking collectives, local(): scores = lax.psum(partial_scores, 'tp')  38.6 us
  transfers between devices with their start and end apart: 25, of which 17 were waited for; matrix products, arithmetic and copies ran while one was open for 9% of the time, Pallas kernels for 0%

profile of v1, /device:TPU:0, one launch (start us, length us, event | category | flops | bytes accessed | tf_op | source)
XLA Modules:
  0.0 884.7 jit_solution(8979634329239232484)
XLA Ops:
  9.5 40.8 %psum.77 = f32[512]{0:T(512)S(1)} all-reduce(f32[512]{0:T(512)S(1)} %fusion.133), channel_id=1, replica_groups=mesh['seq'=8,'tp'=16] {'tp'}, use_global_device_ids=true, to_apply=%region_1.0 | all-reduce | flops 512 | bytes 4096 | tf_op jit(solution)/shard_map/psum | solution.py:91
  66.2 25.8 %all-to-all-done = bf16[16,96,528]{2,1,0:T(8,128)(2,1)} async-done(((bf16[16,96,528]{2,1,0:T(8,128)(2,1)}), bf16[16,96,528]{2,1,0:T(8,128)(2,1)}, u32[]{:S(2)}, u32[]{:S(2)}) %all-to-all-start) | async-done | bytes 1622048 | tf_op jit(solution)/shard_map/all_to_all | solution.py:105
  98.3 37.8 %psum.78 = f32[512]{0:T(512)S(1)} all-reduce(f32[512]{0:T(512)S(1)} %get-tuple-element.50), channel_id=1, replica_groups=mesh['seq'=8,'tp'=16] {'tp'}, use_global_device_ids=true, to_apply=%region_3.0 | all-reduce | flops 512 | bytes 4096 | tf_op jit(solution)/shard_map/psum | solution.py:91
  143.6 4.6 all-to-all-start.1
  149.7 27.6 %all-to-all-done.1 = bf16[16,96,544]{2,1,0:T(8,128)(2,1)} async-done(((bf16[16,96,544]{2,1,0:T(8,128)(2,1)}), bf16[16,96,544]{2,1,0:T(8,128)(2,1)}, u32[]{:S(2)}, u32[]{:S(2)}) %all-to-all-start.1) | async-done | bytes 1671200 | tf_op jit(solution)/shard_map/all_to_all | solution.py:105
  183.8 36.3 %psum.79 = f32[512]{0:T(512)S(1)} all-reduce(f32[512]{0:T(512)S(1)} %get-tuple-element.52), channel_id=1, replica_groups=mesh['seq'=8,'tp'=16] {'tp'}, use_global_device_ids=true, to_apply=%region_5.0 | all-reduce | flops 512 | bytes 4096 | tf_op jit(solution)/shard_map/psum | solution.py:91
  227.7 38.7 %scatter_fusion = s32[8,128]{1,0:T(8,128)} fusion(s32[8,128]{1,0:T(8,128)} %broadcast.156, s32[256]{0:T(256)S(1)} %bitcast.151, s32[256]{0:T(256)} %param.16), kind=kCustom, calls=%fused_computation.3 | custom fusion | bytes 5120 | tf_op jit(solution)/shard_map/scatter | solution.py:114
  266.4 4.6 all-to-all-start.3
  277.7 4.6 all-to-all-start.2
  284.5 27.0 %all-to-all-done.2 = bf16[16,96,576]{2,1,0:T(8,128)(2,1)} async-done(((bf16[16,96,576]{2,1,0:T(8,128)(2,1)}), bf16[16,96,576]{2,1,0:T(8,128)(2,1)}, u32[]{:S(2)}, u32[]{:S(2)}) %all-to-all-start.2) | async-done | bytes 1769504 | tf_op jit(solution)/shard_map/all_to_all | solution.py:105
  319.6 4.6 gather_fusion.1
  344.9 12.3 %scatter_fusion.2 = f32[8,128,96]{2,1,0:T(8,128)S(1)} fusion(f32[8,128,96]{2,1,0:T(8,128)S(1)} %broadcast_in_dim.5, s32[256]{0:T(256)S(1)} %bitcast.152, f32[256,96]{1,0:T(8,128)S(1)} %copy.100), kind=kCustom, calls=%fused_computation.5 | custom fusion | bytes 296960 | tf_op jit(solution)/shard_map/scatter | solution.py:133
  368.3 6.3 scatter_fusion.3
  385.0 71.8 %reduce-scatter.4.cloned.1.call-done = bf16[96,512]{1,0:T(8,128)(2,1)} async-done(((bf16[1536,512]{1,0:T(8,128)(2,1)}), bf16[96,512]{1,0:T(8,128)(2,1)}) %reduce-scatter.4.cloned.1.call-update) | async-done | bytes 98320 | tf_op jit(solution)/shard_map/reduce_scatter | solution.py:152
  458.0 38.2 %psum.81 = f32[512]{0:T(512)S(1)} all-reduce(f32[512]{0:T(512)S(1)} %get-tuple-element.7), channel_id=1, replica_groups=mesh['seq'=8,'tp'=16] {'tp'}, use_global_device_ids=true, to_apply=%region_17.18 | all-reduce | flops 512 | bytes 4096 | tf_op jit(solution)/shard_map/psum | solution.py:172
  512.2 36.9 %all-gather.6.cloned.1.call-done = bf16[1536,544]{1,0:T(8,128)(2,1)} async-done(((bf16[96,544]{1,0:T(8,128)(2,1)}), bf16[1536,544]{1,0:T(8,128)(2,1)}) %all-gather.6.cloned.1.call-update) | async-done | bytes 1671184 | tf_op jit(solution)/shard_map/all_gather | solution.py:164
  554.0 72.6 %reduce-scatter.6.cloned.1.call-done = bf16[96,512]{1,0:T(8,128)(2,1)} async-done(((bf16[1536,512]{1,0:T(8,128)(2,1)}), bf16[96,512]{1,0:T(8,128)(2,1)}) %reduce-scatter.6.cloned.1.call-update) | async-done | bytes 98320 | tf_op jit(solution)/shard_map/reduce_scatter | solution.py:152
  627.9 38.2 %psum.82 = f32[512]{0:T(512)S(1)} all-reduce(f32[512]{0:T(512)S(1)} %get-tuple-element.5), channel_id=1, replica_groups=mesh['seq'=8,'tp'=16] {'tp'}, use_global_device_ids=true, to_apply=%region_20.21 | all-reduce | flops 512 | bytes 4096 | tf_op jit(solution)/shard_map/psum | solution.py:172
  667.3 5.4 all-gather.4.cloned.1.call-done
  686.3 58.8 %all-reduce.4.cloned.1.call-done = (bf16[1,96,3,1536]{3,1,2,0:T(8,128)(2,1)}, bf16[1,96,3,1536]{3,1,2,0:T(8,128)(2,1)}, bf16[1,96,3,1536]{3,1,2,0:T(8,128)(2,1)}) async-done(((bf16[1,96,3,1536]{3,1,2,0:T(8,128)(2,1)}, bf16[1,96,3,1536]{3,1,2,0:T(8,128)(2,1)}, bf16[1,96,3,1536]{3,1,2,0:T(8,128)(2,1)}), (bf16[1,96,3,1536]{3,1,2,0:T(8,128)(2,1)}, bf16[1,96,3,1536]{3,1,2,0:T(8,128)(2,1)}, ...) | async-done | bytes 2654224 | tf_op jit(solution)/shard_map/psum | solution.py:167
  745.1 4.6 maximum_convert_fusion
  749.8 72.6 %reduce-scatter.8.cloned.1.call-done = bf16[96,512]{1,0:T(8,128)(2,1)} async-done(((bf16[1536,512]{1,0:T(8,128)(2,1)}), bf16[96,512]{1,0:T(8,128)(2,1)}) %reduce-scatter.8.cloned.1.call-update) | async-done | bytes 98320 | tf_op jit(solution)/shard_map/reduce_scatter | solution.py:152
  823.7 13.7 %psum.87 = f32[3,96]{1,0:T(4,128)} all-reduce(f32[3,96]{1,0:T(4,128)S(1)} %pad_maximum_fusion.15), channel_id=1, replica_groups=mesh['seq'=8,'tp'=16] {'seq'}, use_global_device_ids=true, to_apply=%region_30.31 | all-reduce | flops 288 | bytes 2304 | tf_op jit(solution)/shard_map/psum | solution.py:178
  837.4 38.6 %all-reduce = (f32[256]{0:T(256)}, f32[512]{0:T(512)S(1)}) all-reduce(f32[256]{0:T(256)S(1)} %broadcast_multiply_fusion.1, f32[512]{0:T(512)S(1)} %get-tuple-element.9), channel_id=1, replica_groups=mesh['seq'=8,'tp'=16] {'tp'}, use_global_device_ids=true, to_apply=%region_11.12 | all-reduce | flops 768 | bytes 6144 | tf_op jit(solution)/shard_map/psum | solution.py:129
  (211 shorter events, 147.3 us)
Async XLA Ops:
  52.0 4.3 collective-permute-start.1
  53.3 3.9 collective-permute-start
  58.7 33.4 %all-to-all-start = ((bf16[16,96,528]{2,1,0:T(8,128)(2,1)}), bf16[16,96,528]{2,1,0:T(8,128)(2,1)}, u32[]{:S(2)}, u32[]{:S(2)}) async-start(bf16[16,96,528]{2,1,0:T(8,128)(2,1)} %stack.64), calls=%async_computation | async-start | bytes 3932160 | tf_op jit(solution)/shard_map/all_to_all | solution.py:105
  136.9 4.3 collective-permute-start.3
  138.2 3.9 collective-permute-start.2
  143.6 33.7 %all-to-all-start.1 = ((bf16[16,96,544]{2,1,0:T(8,128)(2,1)}), bf16[16,96,544]{2,1,0:T(8,128)(2,1)}, u32[]{:S(2)}, u32[]{:S(2)}) async-start(bf16[16,96,544]{2,1,0:T(8,128)(2,1)} %stack.65), calls=%async_computation.1 | async-start | bytes 3932160 | tf_op jit(solution)/shard_map/all_to_all | solution.py:105
  221.5 49.5 %collective-permute-start.5 = (bf16[96,32]{1,0:T(8,128)(2,1)S(1)}, bf16[96,32]{1,0:T(8,128)(2,1)S(1)}, u32[]{:S(2)}, u32[]{:S(2)}) collective-permute-start(bf16[96,32]{1,0:T(8,128)(2,1)S(1)} %get-tuple-element.34), channel_id=1, source_target_pairs={{16,0},{32,16},{48,32},{64,48},{80,64},{96,80},{112,96},{17,1},{33... | collective-permute-start | bytes 18440 | tf_op jit(solution)/shard_map/ppermute | solution.py:21
  222.8 48.8 %collective-permute-start.4 = (bf16[96,32]{1,0:T(8,128)(2,1)S(1)}, bf16[96,32]{1,0:T(8,128)(2,1)}, u32[]{:S(2)}, u32[]{:S(2)}) collective-permute-start(bf16[96,32]{1,0:T(8,128)(2,1)S(1)} %get-tuple-element.33), channel_id=1, source_target_pairs={{0,16},{16,32},{32,48},{48,64},{64,80},{80,96},{96,112},{1,17},{17... | collective-permute-start | bytes 18440 | tf_op jit(solution)/shard_map/ppermute | solution.py:20
  266.4 9.9 %all-to-all-start.3 = ((s32[8,1,128]{2,1,0:T(1,128)}), s32[8,1,128]{2,1,0:T(1,128)S(1)}, u32[]{:S(2)}, u32[]{:S(2)}) async-start(s32[8,1,128]{2,1,0:T(1,128)} %bitcast.30), calls=%async_computation.3 | async-start | bytes 8192 | tf_op jit(solution)/shard_map/all_to_all | solution.py:116
  277.7 33.8 %all-to-all-start.2 = ((bf16[16,96,576]{2,1,0:T(8,128)(2,1)}), bf16[16,96,576]{2,1,0:T(8,128)(2,1)}, u32[]{:S(2)}, u32[]{:S(2)}) async-start(bf16[16,96,576]{2,1,0:T(8,128)(2,1)} %stack.66), calls=%async_computation.2 | async-start | bytes 3932160 | tf_op jit(solution)/shard_map/all_to_all | solution.py:105
  326.0 10.8 %all-to-all-start.4 = ((bf16[8,128,96]{1,2,0:T(8,128)(2,1)}), bf16[8,128,96]{1,2,0:T(8,128)(2,1)}, u32[]{:S(2)}, u32[]{:S(2)}) async-start(bf16[8,128,96]{1,2,0:T(8,128)(2,1)} %copy.95), calls=%async_computation.4 | async-start | bytes 393216 | tf_op jit(solution)/shard_map/all_to_all | solution.py:118
  358.0 10.1 %all-to-all-start.5 = ((bf16[8,128,96]{1,2,0:T(8,128)(2,1)}), bf16[8,128,96]{1,2,0:T(8,128)(2,1)S(1)}, u32[]{:S(2)}, u32[]{:S(2)}) async-start(bf16[8,128,96]{1,2,0:T(8,128)(2,1)} %copy.101), calls=%async_computation.5 | async-start | bytes 393216 | tf_op jit(solution)/shard_map/all_to_all | solution.py:134
  361.4 95.3 %reduce-scatter.4.cloned.1.call-start = ((), (), s32[]{:S(2)}) async-start(), calls=%async_computation.9 | async-start | bytes 1671168 | tf_op jit(solution)/shard_map/reduce_scatter | solution.py:152
  374.7 4.5 collective-permute-start.7
  377.9 3.6 collective-permute-start.6
  383.3 123.7 %all-gather.8.cloned.1.call-start = ((), (), s32[]{:S(2)}) async-start(), calls=%async_computation.14 | async-start | bytes 2088960 | tf_op jit(solution)/shard_map/all_gather | solution.py:164
  384.1 165.0 %all-gather.6.cloned.1.call-start = ((), (), s32[]{:S(2)}) async-start(), calls=%async_computation.13 | async-start | bytes 2088960 | tf_op jit(solution)/shard_map/all_gather | solution.py:164
  384.8 241.8 %reduce-scatter.6.cloned.1.call-start = ((), (), s32[]{:S(2)}) async-start(), calls=%async_computation.10 | async-start | bytes 1671168 | tf_op jit(solution)/shard_map/reduce_scatter | solution.py:152
  497.5 3.2 collective-permute-start.9
  499.5 4.9 collective-permute-start.8
  506.1 166.5 %all-gather.4.cloned.1.call-start = ((), (), s32[]{:S(2)}) async-start(), calls=%async_computation.12 | async-start | bytes 2088960 | tf_op jit(solution)/shard_map/all_gather | solution.py:164
  506.7 238.4 %all-reduce.4.cloned.1.call-start = ((), (), s32[]{:S(2)}) async-start(), calls=%async_computation.15 | async-start | bytes 5308416 | tf_op jit(solution)/shard_map/psum | solution.py:167
  677.6 144.8 %reduce-scatter.8.cloned.1.call-start = ((), (), s32[]{:S(2)}) async-start(), calls=%async_computation.11 | async-start | bytes 1671168 | tf_op jit(solution)/shard_map/reduce_scatter | solution.py:152
  679.6 4.9 collective-permute-start.10
  (39 other events, 2046.6 us)
Sparse Core Ops, SparseCore 0:
  383.4 73.2 reduce-scatter.3
  459.0 43.9 all-gather.7
  505.1 43.9 all-gather.5
  552.7 73.8 reduce-scatter.5
  628.7 43.9 all-gather.3
  677.7 67.3 all-reduce.3
  748.3 73.9 reduce-scatter.7
